TPU v7x, 128 devices: a whole 4x4x4 slice. The times are simulated.
128 devices in a mesh: dom: 64 (over x, y, z), col: 2 (over core).
Axes of the slice: x: 4, y: 4, z: 4, core: 2. Of those that a mesh axis runs over, the one named last changes fastest.
Arguments:
- adjoint_rhs: bfloat16 [12288, 105, 64], P('dom', None, 'col')
- element_blocks: bfloat16 [6144, 420, 420], P('dom', 'col')
- element_faces: int32 [6144, 4], P('dom'), may hold values from 0 to 383, as said below
- send_faces: int32 [64, 192], P('dom'), may hold values from 0 to 191
Outputs:
- second_basis: bfloat16 [12288, 105, 64], P('dom', None, 'col')
- next_vector: bfloat16 [12288, 105, 64], P('dom', None, 'col')
- hessenberg: float32 [5, 64], P(None, 'col')
Inputs may be any that keep to these rules, and one draw needn't show every extreme that they name: `element_faces`: row d * 96 + e belongs to partition d. An entry below 192 is an owned face; an entry 192 + p * 3 + s stands for the face that partition p lists in send_faces at position d * 3 + s. No partition names one of its slots at or above 192 twice, and none names its own index p = d.
All inputs are finite; a program needn't handle non-finite values.
Results may differ from a plain program's by a relative error of at most 0.02.
Values may be sent and summed in bfloat16 or wider, within the bound.
A program may use at most 192 MiB of HBM per device.

v0:
```python
import jax
import jax.numpy as jnp
from jax import lax
from jax.sharding import PartitionSpec as P

P_SIZE = 105


epsilon = 1e-06


def sent_to_all(x, axis):
    peers = lax.axis_size(axis)
    return lax.all_to_all(jnp.broadcast_to(x[None], (peers, *x.shape)), axis, 0, 0, tiled=True)


def joined_along(blocks, dim):
    blocks = jnp.moveaxis(blocks, 0, dim)
    shape = blocks.shape
    return blocks.reshape(*shape[:dim], shape[dim] * shape[dim + 1], *shape[dim + 2 :])


def gather_directly(x, axis, dim):
    blocks = sent_to_all(x, axis)
    return joined_along(blocks, dim)


def cut_along(x, dim, peers):
    shape = x.shape
    blocks = x.reshape(*shape[:dim], peers, shape[dim] // peers, *shape[dim + 1 :])
    return jnp.moveaxis(blocks, dim, 0)


def sum_at_owner(x, axis, dim):
    blocks = cut_along(x, dim, lax.axis_size(axis))
    arrived = lax.all_to_all(blocks, axis, split_axis=0, concat_axis=0, tiled=True)
    return arrived.astype(jnp.float32).sum(axis=0)


def over_copies(x, axis):
    return sent_to_all(x, axis).sum(axis=0)


def together(arrays, axis):
    flat, at, gathered = (jnp.concatenate([a.reshape(-1) for a in arrays]), 0, [])
    total = over_copies(flat, axis)
    for a in arrays:
        gathered.append(total[at : at + a.size].reshape(a.shape))
        at += a.size
    return tuple(gathered)


def body(adjoint_rhs, element_blocks, element_faces, send_faces):
    owned_count = adjoint_rhs.shape[0]
    dom_ranks = lax.axis_size("dom")
    entries = float(dom_ranks * owned_count * P_SIZE)
    outgoing_faces = send_faces[0]
    ghost_count = outgoing_faces.shape[0]
    slot_share = element_blocks.shape[1] // P_SIZE
    slot_total = element_blocks.shape[2] // P_SIZE
    element_count = element_blocks.shape[0]
    first_slot = lax.axis_index("col") * slot_share
    chosen_slots = lax.dynamic_slice_in_dim(element_faces, first_slot, slot_share, 1)
    all_slots = element_faces.reshape(-1)

    def transposed(vector_half):
        full_traces = gather_directly(vector_half, "col", 2)
        incoming = lax.all_to_all(
            full_traces[outgoing_faces], "dom", split_axis=0, concat_axis=0, tiled=True
        )
        known_traces = jnp.concatenate([full_traces, incoming], axis=0)
        picked = known_traces[chosen_slots].reshape(
            element_count, slot_share * P_SIZE, known_traces.shape[2]
        )
        partial_terms = jnp.einsum(
            "ekb,ekr->ebr", element_blocks, picked, preferred_element_type=jnp.float32
        )
        summed = jax.ops.segment_sum(
            partial_terms.reshape(element_count * slot_total, P_SIZE, known_traces.shape[2]),
            all_slots,
            num_segments=owned_count + ghost_count,
        )
        reduced = sum_at_owner(summed.astype(jnp.bfloat16), "col", 2)
        returned = lax.all_to_all(
            reduced[owned_count:].astype(jnp.bfloat16),
            "dom",
            split_axis=0,
            concat_axis=0,
            tiled=True,
        ).astype(jnp.float32)
        return reduced[:owned_count] + jax.ops.segment_sum(
            returned, outgoing_faces, num_segments=owned_count
        )

    residual = adjoint_rhs.astype(jnp.float32)
    start_norm = jnp.sqrt(
        over_copies(jnp.sum(residual * residual, axis=(0, 1)), "dom") / entries + epsilon
    )
    first_basis = (residual / start_norm).astype(jnp.bfloat16)
    first_image = transposed(first_basis)
    first_float = first_basis.astype(jnp.float32)
    diagonal_term = over_copies(jnp.sum(first_float * first_image, axis=(0, 1)), "dom") / entries
    projected = first_image - diagonal_term * first_float
    next_norm = jnp.sqrt(
        over_copies(jnp.sum(projected * projected, axis=(0, 1)), "dom") / entries + epsilon
    )
    second_basis = (projected / next_norm).astype(jnp.bfloat16)
    second_image = transposed(second_basis)
    second_float = second_basis.astype(jnp.float32)
    first_total, second_total = together(
        (
            jnp.sum(first_float * second_image, axis=(0, 1)),
            jnp.sum(second_float * second_image, axis=(0, 1)),
        ),
        "dom",
    )
    proj_first = first_total / entries
    proj_second = second_total / entries
    next_vector = (second_image - proj_first * first_float - proj_second * second_float).astype(
        jnp.bfloat16
    )
    hessenberg = jnp.stack([start_norm, diagonal_term, next_norm, proj_first, proj_second])
    return (second_basis, next_vector, hessenberg)


def solution(mesh):
    in_specs = (P("dom", None, "col"), P("dom", "col", None), P("dom", None), P("dom", None))
    out_specs = (P("dom", None, "col"), P("dom", None, "col"), P(None, "col"))
    return jax.shard_map(body, mesh=mesh, in_specs=in_specs, out_specs=out_specs, check_vma=False)
```

profile of v0, /device:TPU:0, one launch (start us, length us, event | category | flops | bytes accessed | tf_op | source)
XLA Modules:
  0.0 660.2 jit_solution(16187196920174749110)
XLA Ops:
  3.2 11.5 %all-to-all-start = ((f32[64,1,32]{2,1,0:T(1,128)}), f32[64,1,32]{2,1,0:T(1,128)S(1)}, u32[]{:S(2)}, u32[]{:S(2)}) async-start(f32[64,1,32]{2,1,0:T(1,128)} %broadcast_in_dim.14), calls=%async_computation | async-start | bytes 65536 | tf_op jit(solution)/shard_map/all_to_all | solution.py:14
  43.5 31.7 %copy.105 = bf16[96,210,420]{1,2,0:T(8,128)(2,1)} copy(bf16[96,210,420]{2,0,1:T(8,128)(2,1)} %param.5) | data formatting | bytes 33868800 | tf_op args[1]
  102.4 12.9 %convolution_bitcast_fusion.1 = f32[96,420,64]{1,2,0:T(8,128)} fusion(bf16[96,210,420]{1,2,0:T(8,128)(2,1)} %copy.105, bf16[96,210,64]{1,0,2:T(8,128)(2,1)S(1)} %reshape.145), kind=kOutput, calls=%fused_computation.17 | convolution fusion | flops 1083801600 | bytes 29836800 | tf_op jit(solution)/shard_map/ekb,ekr->ebr/dot_general | solution.py:75
  115.4 16.3 %copy.106 = f32[96,420,64]{1,0,2:T(8,128)} copy(f32[96,420,64]{1,2,0:T(8,128)} %convolution_bitcast_fusion.1) | data formatting | bytes 20643840 | tf_op jit(solution)/shard_map/ekb,ekr->ebr/dot_general | solution.py:75
  131.7 14.8 %reshape.188 = f32[384,105,64]{1,0,2:T(8,128)} reshape(f32[96,420,64]{1,0,2:T(8,128)} %copy.106) | data formatting | bytes 20643840 | tf_op jit(solution)/shard_map/reshape | solution.py:79
  146.5 16.3 %copy.107 = f32[384,105,64]{1,2,0:T(8,128)} copy(f32[384,105,64]{1,0,2:T(8,128)} %reshape.188) | data formatting | bytes 20643840 | tf_op jit(solution)/shard_map/reshape | solution.py:79
  169.0 59.4 %scatter_fusion = f32[384,105,64]{1,2,0:T(8,128)} fusion(f32[384,105,64]{1,2,0:T(8,128)} %broadcast.119.clone, s32[384]{0:T(512)S(1)} %reshape.186, f32[384,105,64]{1,2,0:T(8,128)} %copy.107), kind=kCustom, calls=%fused_computation.4 | custom fusion | flops 2580480 | bytes 30967296 | tf_op jit(solution)/shard_map/scatter-add | solution.py:78
  237.3 9.6 %copy.108 = bf16[384,105,2,32]{0,3,1,2:T(8,128)(2,1)} copy(bf16[384,105,2,32]{1,3,2,0:T(8,128)(2,1)} %bitcast.43) | data formatting | bytes 10321920 | tf_op jit(solution)/shard_map/reshape | solution.py:30
  246.9 9.5 %all_to_all.65 = bf16[2,384,105,32]{1,3,2,0:T(8,128)(2,1)S(1)} all-to-all(bf16[2,384,105,32]{1,3,2,0:T(8,128)(2,1)} %bitcast.45), channel_id=1, replica_groups=mesh['dom'=64,'col'=2] {'col'}, dimensions={0} | all-to-all | bytes 10321920 | tf_op jit(solution)/shard_map/all_to_all | solution.py:36
  280.9 16.2 %all-to-all-done.4 = bf16[192,105,32]{1,2,0:T(8,128)(2,1)} async-done(((bf16[192,105,32]{1,2,0:T(8,128)(2,1)}), bf16[192,105,32]{1,2,0:T(8,128)(2,1)}, u32[]{:S(2)}, u32[]{:S(2)}) %all-to-all-start.4) | async-done | bytes 1290272 | tf_op jit(solution)/shard_map/all_to_all | solution.py:84
  300.7 17.2 %scatter_fusion.1 = f32[192,105,32]{1,2,0:T(8,128)S(1)} fusion(f32[192,105,32]{1,2,0:T(8,128)S(1)} %copy.126, s32[192]{0:T(256)S(1)} %bitcast.48, f32[192,105,32]{1,2,0:T(8,128)} %convert_element_type.42), kind=kCustom, calls=%fused_computation.5 | custom fusion | flops 645120 | bytes 7742208 | tf_op jit(solution)/shard_map/scatter-add | solution.py:91
  320.1 14.0 %all_to_all.69 = f32[64,1,32]{2,1,0:T(1,128)S(1)} all-to-all(f32[64,1,32]{2,1,0:T(1,128)S(1)} %broadcast_in_dim.17), channel_id=1, replica_groups=mesh['dom'=64,'col'=2] {'dom'}, dimensions={0} | all-to-all | bytes 16384 | tf_op jit(solution)/shard_map/all_to_all | solution.py:14
  336.6 14.3 %all_to_all.70 = f32[64,1,32]{2,1,0:T(1,128)S(1)} all-to-all(f32[64,1,32]{2,1,0:T(1,128)S(1)} %broadcast_in_dim.18), channel_id=1, replica_groups=mesh['dom'=64,'col'=2] {'dom'}, dimensions={0} | all-to-all | bytes 16384 | tf_op jit(solution)/shard_map/all_to_all | solution.py:14
  363.7 46.6 %all_to_all.67 = bf16[192,105,64]{1,2,0:T(8,128)(2,1)S(1)} all-to-all(bf16[192,105,64]{1,2,0:T(8,128)(2,1)} %gather_fusion.2), channel_id=1, replica_groups=mesh['dom'=64,'col'=2] {'dom'}, dimensions={0} | all-to-all | bytes 5160960 | tf_op jit(solution)/shard_map/all_to_all | solution.py:68
  426.2 13.1 %convolution_bitcast_fusion = f32[96,420,64]{1,2,0:T(8,128)} fusion(bf16[96,210,420]{1,2,0:T(8,128)(2,1)} %copy.105, bf16[96,210,64]{1,0,2:T(8,128)(2,1)S(1)} %reshape.149), kind=kOutput, calls=%fused_computation.16 | convolution fusion | flops 1083801600 | bytes 29836800 | tf_op jit(solution)/shard_map/ekb,ekr->ebr/dot_general | solution.py:75
  439.3 16.4 %copy.117 = f32[96,420,64]{1,0,2:T(8,128)} copy(f32[96,420,64]{1,2,0:T(8,128)} %convolution_bitcast_fusion) | data formatting | bytes 20643840 | tf_op jit(solution)/shard_map/ekb,ekr->ebr/dot_general | solution.py:75
  455.7 14.5 %reshape.204 = f32[384,105,64]{1,0,2:T(8,128)} reshape(f32[96,420,64]{1,0,2:T(8,128)} %copy.117) | data formatting | bytes 20643840 | tf_op jit(solution)/shard_map/reshape | solution.py:79
  470.2 16.4 %copy.118 = f32[384,105,64]{1,2,0:T(8,128)} copy(f32[384,105,64]{1,0,2:T(8,128)} %reshape.204) | data formatting | bytes 20643840 | tf_op jit(solution)/shard_map/reshape | solution.py:79
  492.7 59.4 %scatter_fusion.2 = f32[384,105,64]{1,2,0:T(8,128)} fusion(f32[384,105,64]{1,2,0:T(8,128)} %broadcast.119, s32[384]{0:T(512)S(1)} %reshape.186, f32[384,105,64]{1,2,0:T(8,128)} %copy.118), kind=kCustom, calls=%fused_computation.6 | custom fusion | flops 2580480 | bytes 30967296 | tf_op jit(solution)/shard_map/scatter-add | solution.py:78
  561.1 9.7 %copy.119 = bf16[384,105,2,32]{0,3,1,2:T(8,128)(2,1)} copy(bf16[384,105,2,32]{1,3,2,0:T(8,128)(2,1)} %bitcast.44) | data formatting | bytes 10321920 | tf_op jit(solution)/shard_map/reshape | solution.py:30
  570.8 9.5 %all_to_all.68 = bf16[2,384,105,32]{1,3,2,0:T(8,128)(2,1)S(1)} all-to-all(bf16[2,384,105,32]{1,3,2,0:T(8,128)(2,1)} %bitcast.46), channel_id=1, replica_groups=mesh['dom'=64,'col'=2] {'col'}, dimensions={0} | all-to-all | bytes 10321920 | tf_op jit(solution)/shard_map/all_to_all | solution.py:36
  601.1 16.4 %all-to-all-done.10 = bf16[192,105,32]{1,2,0:T(8,128)(2,1)} async-done(((bf16[192,105,32]{1,2,0:T(8,128)(2,1)}), bf16[192,105,32]{1,2,0:T(8,128)(2,1)}, u32[]{:S(2)}, u32[]{:S(2)}) %all-to-all-start.10) | async-done | bytes 1290272 | tf_op jit(solution)/shard_map/all_to_all | solution.py:84
  621.0 17.2 %scatter_fusion.3 = f32[192,105,32]{1,2,0:T(8,128)S(1)} fusion(f32[192,105,32]{1,2,0:T(8,128)S(1)} %copy.127, s32[192]{0:T(256)S(1)} %bitcast.49, f32[192,105,32]{1,2,0:T(8,128)} %convert_element_type.47), kind=kCustom, calls=%fused_computation.7 | custom fusion | flops 645120 | bytes 7742208 | tf_op jit(solution)/shard_map/scatter-add | solution.py:91
  641.3 14.0 %all_to_all.71 = f32[64,1,64]{2,1,0:T(1,128)S(1)} all-to-all(f32[64,1,64]{2,1,0:T(1,128)S(1)} %broadcast_in_dim.20), channel_id=1, replica_groups=mesh['dom'=64,'col'=2] {'dom'}, dimensions={0} | all-to-all | bytes 32768 | tf_op jit(solution)/shard_map/all_to_all | solution.py:14
  (78 shorter events, 181.8 us)
Async XLA Ops:
  3.2 21.0 %all-to-all-start = ((f32[64,1,32]{2,1,0:T(1,128)}), f32[64,1,32]{2,1,0:T(1,128)S(1)}, u32[]{:S(2)}, u32[]{:S(2)}) async-start(f32[64,1,32]{2,1,0:T(1,128)} %broadcast_in_dim.14), calls=%async_computation | async-start | bytes 65536 | tf_op jit(solution)/shard_map/all_to_all | solution.py:14
  37.2 5.9 copy-start.4
  37.2 47.4 %all-to-all-start.2 = ((bf16[192,105,64]{1,2,0:T(8,128)(2,1)}), bf16[192,105,64]{1,2,0:T(8,128)(2,1)}, u32[]{:S(2)}, u32[]{:S(2)}) async-start(bf16[192,105,64]{1,2,0:T(8,128)(2,1)} %gather_fusion), calls=%async_computation.2 | async-start | bytes 6291456 | tf_op jit(solution)/shard_map/all_to_all | solution.py:68
  257.3 2.3 copy-start.1
  263.4 33.8 %all-to-all-start.4 = ((bf16[192,105,32]{1,2,0:T(8,128)(2,1)}), bf16[192,105,32]{1,2,0:T(8,128)(2,1)}, u32[]{:S(2)}, u32[]{:S(2)}) async-start(bf16[192,105,32]{1,2,0:T(8,128)(2,1)} %copy.110), calls=%async_computation.4 | async-start | bytes 3145728 | tf_op jit(solution)/shard_map/all_to_all | solution.py:84
  280.9 19.8 %copy-start.3 = (s32[1,192]{1,0:T(1,128)S(1)}, s32[1,192]{1,0:T(1,128)}, u32[]{:S(2)}) copy-start(s32[1,192]{1,0:T(1,128)} %param.7) | copy-start | bytes 2308
  353.2 6.7 %copy-start = (bf16[192,105,32]{1,2,0:T(8,128)(2,1)}, bf16[192,105,32]{1,2,0:T(8,128)(2,1)S(1)}, u32[]{:S(2)}) copy-start(bf16[192,105,32]{1,2,0:T(8,128)(2,1)S(1)} %divide_convert_fusion) | copy-start | bytes 3870724
  581.2 2.3 copy-start.2
  587.3 30.2 %all-to-all-start.10 = ((bf16[192,105,32]{1,2,0:T(8,128)(2,1)}), bf16[192,105,32]{1,2,0:T(8,128)(2,1)}, u32[]{:S(2)}, u32[]{:S(2)}) async-start(bf16[192,105,32]{1,2,0:T(8,128)(2,1)} %copy.121), calls=%async_computation.10 | async-start | bytes 3145728 | tf_op jit(solution)/shard_map/all_to_all | solution.py:84
  655.4 3.9 copy-start.5
where the time goes:
time: 670 us; the launch traced here: 660 us
  local copies, waits for them, and re-layouts  221 us (33%)
  other arithmetic  209 us (31%)
  blocking collectives  120 us (18%)
  waiting for transfers between devices  50.7 us (8%)
  starting transfers between devices  32.5 us (5%)
  matrix products  26 us (4%)
    scatter-add x2, other arithmetic, transposed(): jax.ops.segment_sum(partial_terms.reshape(element_count * slot_total, P_S...  119 us
    reshape x4, local copies, waits for them, and re-layouts, transposed(): partial_terms.reshape(element_count * slot_total, P_SIZE, known_traces.sh...  62.1 us
    all_to_all x5, blocking collectives, sent_to_all(): lax.all_to_all(jnp.broadcast_to(x[None], (peers, *x.shape)), axis, 0, 0,...  54.9 us
    all_to_all x1, blocking collectives, transposed(): lax.all_to_all(full_traces[outgoing_faces], 'dom', split_axis=0, concat_a...  46.6 us
    unnamed x16, local copies, waits for them, and re-layouts  44.3 us
    scatter-add x2, other arithmetic, transposed(): jax.ops.segment_sum(returned, outgoing_faces, num_segments=owned_count)  34.5 us
    dot_general x2, local copies, waits for them, and re-layouts, transposed(): jnp.einsum('ekb,ekr->ebr', element_blocks, picked, preferred_element_type...  32.8 us
    all_to_all x2, waiting for transfers between devices, transposed(): lax.all_to_all(reduced[owned_count:].astype(jnp.bfloat16), 'dom', split_a...  32.6 us
  transfers between devices with their start and end apart: 4, of which 4 were waited for; matrix products, arithmetic and copies ran while one was open for 7% of the time, Pallas kernels for 0%

commit v1 on v0

v1 whole, which is shorter than its diff:
```python
import jax
import jax.numpy as jnp
from jax import lax
from jax.experimental import pallas as pl
from jax.experimental.pallas import tpu as pltpu
from jax.sharding import PartitionSpec as P

P_SIZE = 105
EPS = 1e-06
MESH = pl.DeviceIdType.MESH
NDOM = 64
ELEMS = 96
OWNED = 192
SLOT = 3
HALF = 32
WIRE = 80
STEP = 27
ENTRIES = float(NDOM * OWNED * P_SIZE)
F32 = jnp.float32
BF16 = jnp.bfloat16
VMEM_LIMIT = 67043328
GROUP = 8
PARTS = 8


def lanes(rows):
    return lax.broadcasted_iota(jnp.int32, (rows, 128), 1)


def rows_of(rows):
    return lax.broadcasted_iota(jnp.int32, (rows, 128), 0)


def pack(f0, f1, f2):
    lane = lanes(16)
    tail = f2[16:]
    out = []
    for j, part in enumerate((f0[:16], f0[16:], f1[:16], f1[16:], f2[:16])):
        moved = pltpu.roll(tail, 105 - 21 * j, 1)
        out.append(jnp.where(lane < 105, part, jnp.where(lane < 126, moved, 0.0)))
    return jnp.concatenate(out, axis=0)


def unpack(message):
    lane = lanes(16)
    tail = jnp.zeros((16, 128), F32)
    parts = []
    for j in range(5):
        part = message[16 * j : 16 * j + 16]
        moved = pltpu.roll(part, 128 - (105 - 21 * j), 1)
        tail = jnp.where((lane >= 21 * j) & (lane < 21 * j + 21), moved, tail)
        parts.append(jnp.where(lane < 105, part, 0.0))
    cat = lambda a, b: jnp.concatenate([a, b], axis=0)
    return cat(parts[0], parts[1]), cat(parts[2], parts[3]), cat(parts[4], tail)


def to_lanes(column):
    return jnp.sum(jnp.where(rows_of(HALF) == lanes(HALF), column, 0.0), axis=0, keepdims=True)


def to_rows(row):
    return jnp.sum(jnp.where(rows_of(HALF) == lanes(HALF), row, 0.0), axis=1, keepdims=True)


def lane_sum(x):
    return jnp.sum(x, axis=1, keepdims=True)


def relayout(a, o_ref, e0):
    group = GROUP
    at = pl.ds(e0, group)
    for s in range(2):
        for k in range(0, 105, 16):
            n = min(16, 105 - k)
            x = a[s * 105 + k : s * 105 + k + n]
            if n < 16:
                x = jnp.concatenate([x, jnp.zeros((16 - n, group, 420), x.dtype)], 0)
            y = jnp.swapaxes(x, 0, 1)
            for b in range(4):
                z = jnp.concatenate(
                    [y[:, :, 105 * b : 105 * b + 105], jnp.zeros((group, 16, 23), y.dtype)], -1
                )
                o_ref[at, s * 128 + k : s * 128 + k + 16, b * 128 : b * 128 + 128] = z
        o_ref[at, s * 128 + 112 : s * 128 + 128, :] = jnp.zeros((group, 16, 512), o_ref.dtype)


def offset(k):
    return lax.rem(k * STEP, NDOM)


def loop(first, last, body, unroll=1):
    def step(k, _):
        body(k)
        return 0

    lax.fori_loop(first, last, step, 0, unroll=unroll)


def each(body, unroll=1):
    loop(1, NDOM, body, unroll)


def remote(source, target, send, recv, d, c):
    return pltpu.make_async_remote_copy(
        source, target, send, recv, device_id=(d, c), device_id_type=MESH
    )


def to_f32(x):
    return x.astype(F32)


def whole_kernel(
    send_ref, faces_ref, prev_ref, last_ref, prev2_ref, last2_ref, r_ref, a_hbm,
    basis_hbm, next_hbm, h_ref,
    blocks, known, sums, b1, wire, ghost, ghost2, keep, give, got, keepg, giveg, gotg, ret,
    stat, stats, staging,
    a_sem, hsend, hrecv, fsend, frecv, ssend, srecv, xsend, xrecv, rsend, rrecv, pair_sem, sem,
):
    d, c = lax.axis_index("dom"), lax.axis_index("col")
    other = 1 - c
    low, high = pl.ds(0, HALF), pl.ds(HALF, HALF)
    owned = pl.ds(0, OWNED)
    zero = jnp.zeros((HALF, 128), F32)

    def target(k):
        return lax.rem(d + offset(k), NDOM)

    def source(k):
        return lax.rem(d - offset(k) + NDOM, NDOM)

    def load(g):
        slot = lax.rem(g, 2)
        part = a_hbm.at[:, pl.ds(pl.multiple_of(g * GROUP, GROUP), GROUP), :]
        return pltpu.make_async_copy(part, staging.at[slot], a_sem.at[slot])

    def stat_copy(i, k):
        return remote(stat, stats.at[i, d], ssend.at[k], srecv.at[k], target(k), c)

    def spread(i):
        mine = pltpu.make_async_copy(stat, stats.at[i, d], sem.at[0])
        mine.start()
        each(lambda k: stat_copy(i, k).start())
        mine.wait()

    def gathered(i):
        each(lambda k: stat_copy(i, k).wait())

    def send_copy(k):
        return remote(wire.at[target(k)], ghost.at[d], hsend.at[k], hrecv.at[k], target(k), c)

    def forward(k):
        s = source(k)
        return remote(ghost.at[s], ghost2.at[s], fsend.at[k], frecv.at[k], d, other)

    def across():
        return remote(
            known.at[owned, low], known.at[owned, high], pair_sem.at[0], pair_sem.at[1], d, other
        )

    def cross(i):
        part = pl.ds(i * (NDOM // PARTS), NDOM // PARTS)
        return remote(giveg.at[part], gotg.at[part], xsend.at[i], xrecv.at[i], d, other)

    def give_copy():
        return remote(give, got, pair_sem.at[2], pair_sem.at[3], d, other)

    def back(k):
        return remote(keepg.at[k], ret.at[d], rsend.at[k], rrecv.at[k], target(k), c)

    def pack_faces(face):
        def step(p):
            faces = [face(send_ref[SLOT * p + s]) for s in range(SLOT)]
            wire[p] = pack(*faces).astype(BF16)

        loop(0, NDOM, step, 4)

    def fill(s, source_ref, half):
        for j, face in enumerate(unpack(to_f32(source_ref[s]))):
            known[OWNED + SLOT * s + j, half * HALF : half * HALF + HALF] = face.astype(BF16)

    def arrive(k):
        send_copy(k).wait_recv()
        forward(k).start()
        fill(source(k), ghost, 0)

    def halo_end():
        def step(k):
            forward(k).wait_recv()
            fill(source(k), ghost2, 1)

        each(step, 3)

        def done(k):
            send_copy(k).wait_send()
            forward(k).wait_send()

        each(done)
        across().wait()

    def apply():
        first = 2 * c
        sums[4 * ELEMS] = jnp.zeros((2 * HALF, 128), F32)

        def element(e):
            at = 4 * e
            x = jnp.concatenate(
                [known[faces_ref[at + first]], known[faces_ref[at + first + 1]]], axis=1
            )
            y = jnp.dot(x, blocks[e], preferred_element_type=F32)
            for b in range(4):
                sums[at + b] = y[:, 128 * b : 128 * b + 128] + sums[prev_ref[at + b]]

        loop(0, ELEMS, element, 8)
        size = NDOM // PARTS

        def part(i):
            def one(j):
                k = i * size + j
                p = target(k)
                t = [sums[last_ref[OWNED + SLOT * p + s]] for s in range(SLOT)]
                keepg[k] = pack(*(x[:HALF] for x in t)).astype(BF16)
                giveg[k] = pack(*(x[HALF:] for x in t)).astype(BF16)

            loop(0, size, one, 4)

            @pl.when(i > 0)
            def _():
                cross(i - 1).start()

        loop(0, PARTS, part)

        def take(f):
            total = sums[last_ref[f]].astype(BF16)
            keep[f] = total[:HALF]
            give[f] = total[HALF:]

        loop(0, OWNED, take, 8)
        cross(PARTS - 1).start()
        give_copy().start()

        def pass_on(i):
            cross(i).wait_recv()

            def one(j):
                k = i * size + j
                keepg[k] = (to_f32(keepg[k]) + to_f32(gotg[k])).astype(BF16)

            loop(0, size, one, 4)

            def go(j):
                @pl.when(i + j > 0)
                def _():
                    back(i * size + j).start()

            loop(0, size, go)

        loop(0, PARTS, pass_on)

    def add_returned(image):
        give_copy().wait()
        loop(0, PARTS, lambda i: cross(i).wait_send())
        each(lambda k: back(k).wait())
        sums[OWNED, :HALF] = zero

        def step(p):
            for s, face in enumerate(unpack(to_f32(ret[p]))):
                at = SLOT * p + s
                sums[at, :HALF] = face + sums[prev2_ref[at], :HALF]

        loop(0, NDOM, step, 4)

        def own(f, carry):
            value = to_f32(keep[f]) + to_f32(got[f]) + sums[last2_ref[f], :HALF]
            return image(f, value, carry)

        return lax.fori_loop(0, OWNED, own, (zero, zero), unroll=8)

    def stat_rows(*columns):
        stat[...] = jnp.zeros((8, 128), F32)
        for row, x in enumerate(columns):
            stat[row : row + 1] = to_lanes(lane_sum(x))

    def stat_of(i, row):
        return stats[i, :, row, :]

    def total_of(i, row):
        return jnp.sum(stat_of(i, row), axis=0, keepdims=True)

    load(0).start()
    load(1).start()
    barrier = pltpu.get_barrier_semaphore()
    each(
        lambda k: pl.semaphore_signal(
            barrier, inc=1, device_id=(target(k), c), device_id_type=MESH
        )
    )
    pl.semaphore_signal(barrier, inc=1, device_id=(d, other), device_id_type=MESH)

    def right_side(f):
        return jnp.concatenate([to_f32(r_ref[f]), jnp.zeros((HALF, 128 - P_SIZE), F32)], 1)

    def enter(f, total):
        x = right_side(f)
        known[f, :HALF] = x.astype(BF16)
        return total + x * x

    stat_rows(lax.fori_loop(0, OWNED, enter, zero, unroll=8))
    pack_faces(right_side)
    pl.semaphore_wait(barrier, NDOM)

    each(lambda k: send_copy(k).start())
    across().start()
    spread(0)
    ahead = ELEMS // GROUP - 8

    def order(g):
        load(g).wait()
        relayout(staging.at[lax.rem(g, 2)], blocks, g * GROUP)

        @pl.when(g + 2 < ELEMS // GROUP)
        def _():
            load(g + 2).start()

        @pl.when(g >= ahead)
        def _():
            def one(j):
                k = (g - ahead) * 8 + j

                @pl.when(k > 0)
                def _():
                    arrive(k)

            loop(0, 8, one)

    loop(0, ELEMS // GROUP, order)
    halo_end()
    gathered(0)
    apply()
    start_norm = jnp.sqrt(total_of(0, 0) / ENTRIES + EPS)
    scale = 1.0 / to_rows(start_norm)

    def first_image(f, value, carry):
        u = value * scale
        b = (to_f32(known[f, :HALF]) * scale).astype(BF16)
        sums[f, HALF:] = u
        b1[f] = b
        b = to_f32(b)
        return carry[0] + b * b, carry[1] + b * u

    bb, bu = add_returned(first_image)
    local = lane_sum(bb)
    local = lane_sum(bu) / jnp.where(local > 0.0, local, 1.0)

    def square(f, total):
        off = sums[f, HALF:] - local * to_f32(b1[f])
        return total + off * off

    stat_rows(bb, bu, lax.fori_loop(0, OWNED, square, zero, unroll=8))
    spread(1)
    gathered(1)
    diagonal = total_of(1, 1) / ENTRIES
    bb = stat_of(1, 0)
    off = stat_of(1, 1) / jnp.where(bb > 0.0, bb, 1.0) - diagonal
    squares = jnp.sum(stat_of(1, 2) + off * off * bb, axis=0, keepdims=True)
    next_norm = jnp.sqrt(squares / ENTRIES + EPS)
    slope, scale2 = to_rows(diagonal), 1.0 / to_rows(next_norm)

    def second_basis(f):
        b = ((sums[f, HALF:] - slope * to_f32(b1[f])) * scale2).astype(BF16)
        known[f, :HALF] = b
        keep[f] = b

    loop(0, OWNED, second_basis, 8)
    pack_faces(lambda f: to_f32(keep[f]))
    across().start()
    each(lambda k: send_copy(k).start())
    basis = pltpu.make_async_copy(known.at[owned, low], basis_hbm, sem.at[1])
    basis.start()
    each(arrive, 3)
    halo_end()
    apply()

    def second_image(f, value, carry):
        sums[f, HALF:] = value
        return carry[0] + to_f32(b1[f]) * value, carry[1] + to_f32(known[f, :HALF]) * value

    stat_rows(*add_returned(second_image))
    spread(2)
    gathered(2)
    first_row, second_row = total_of(2, 0) / ENTRIES, total_of(2, 1) / ENTRIES
    h_ref[...] = jnp.zeros((8, 128), F32)
    for i, row in enumerate((start_norm, diagonal, next_norm, first_row, second_row)):
        h_ref[i : i + 1] = row
    p1, p2 = to_rows(first_row), to_rows(second_row)

    def last_vector(f):
        out = sums[f, HALF:] - p1 * to_f32(b1[f]) - p2 * to_f32(known[f, :HALF])
        keep[f] = out.astype(BF16)

    loop(0, OWNED, last_vector, 8)
    vector = pltpu.make_async_copy(keep, next_hbm, sem.at[2])
    vector.start()
    vector.wait()
    basis.wait()


def sems(n):
    return pltpu.SemaphoreType.DMA((n,))


def whole(scalars, r, blocks):
    faces, message = (OWNED, HALF, 128), (NDOM, WIRE, 128)
    vm = lambda shape, kind=BF16: pltpu.VMEM(shape, kind)
    return pl.pallas_call(
        whole_kernel,
        in_specs=[pl.BlockSpec(memory_space=pltpu.SMEM)] * len(scalars)
        + [pl.BlockSpec(memory_space=pltpu.VMEM), pl.BlockSpec(memory_space=pl.ANY)],
        out_specs=[pl.BlockSpec(memory_space=pl.ANY)] * 2
        + [pl.BlockSpec(memory_space=pltpu.VMEM)],
        out_shape=[
            jax.ShapeDtypeStruct(faces, BF16),
            jax.ShapeDtypeStruct(faces, BF16),
            jax.ShapeDtypeStruct((8, 128), F32),
        ],
        scratch_shapes=[
            vm((ELEMS, 256, 512)),
            vm((2 * OWNED, 2 * HALF, 128)),
            vm((4 * ELEMS + 1, 2 * HALF, 128), F32),
            vm(faces),
            vm(message), vm(message), vm(message),
            vm(faces), vm(faces), vm(faces),
            vm(message), vm(message), vm(message), vm(message),
            vm((8, 128), F32),
            vm((3, NDOM, 8, 128), F32),
            vm((2, 210, GROUP, 420)),
        ]
        + [sems(2)] + [sems(NDOM)] * 6 + [sems(PARTS)] * 2 + [sems(NDOM)] * 2 + [sems(4), sems(3)],
        compiler_params=pltpu.CompilerParams(
            collective_id=0, has_side_effects=True, vmem_limit_bytes=VMEM_LIMIT
        ),
    )(*scalars, r, blocks)


def latest(names, queries, before, usable, empty):
    j = jnp.arange(names.shape[0], dtype=jnp.int32)
    match = (names[None, :] == queries[:, None]) & (j[None, :] < before[:, None]) & usable[None, :]
    best = jnp.max(jnp.where(match, j[None, :], -1), axis=1)
    return jnp.where(best < 0, empty, best)


def body(adjoint_rhs, element_blocks, element_faces, send_faces):
    d = lax.axis_index("dom")
    faces = element_faces.reshape(-1)
    send = send_faces[0]
    slots = jnp.arange(2 * OWNED, dtype=jnp.int32)
    at = jnp.arange(faces.shape[0], dtype=jnp.int32)
    full = jnp.full((2 * OWNED,), 2 * OWNED, jnp.int32)
    every = jnp.ones((faces.shape[0],), bool)
    found = latest(
        faces, jnp.concatenate([faces, slots]), jnp.concatenate([at, full]), every, 4 * ELEMS
    )
    owned = slots[:OWNED]
    found2 = latest(
        send, jnp.concatenate([send, owned]), jnp.concatenate([owned, full[:OWNED]]),
        owned // SLOT != d, OWNED,
    )
    scalars = (
        send, faces, found[: 4 * ELEMS], found[4 * ELEMS :], found2[:OWNED], found2[OWNED:],
    )
    basis, vector, rows = whole(
        scalars, jnp.transpose(adjoint_rhs, (0, 2, 1)), jnp.transpose(element_blocks, (1, 0, 2))
    )
    out = lambda x: jnp.transpose(x[:, :, :P_SIZE], (0, 2, 1))
    return out(basis), out(vector), rows[:5, :HALF]


def solution(mesh):
    in_specs = (P("dom", None, "col"), P("dom", "col", None), P("dom", None), P("dom", None))
    out_specs = (P("dom", None, "col"), P("dom", None, "col"), P(None, "col"))
    return jax.shard_map(body, mesh=mesh, in_specs=in_specs, out_specs=out_specs, check_vma=False)
```

time: 670 us -> 158 us (0.24); the launches traced: 660 us -> 157 us
  local copies, waits for them, and re-layouts: 221 us -> 7.38 us
  other arithmetic: 209 us -> 2.74 us
  Pallas kernels: 0 us -> 146 us
  blocking collectives: 120 us -> 0 us
  waiting for transfers between devices: 50.7 us -> 0 us
  starting transfers between devices: 32.5 us -> 0 us
  matrix products: 26 us -> 0 us
    scatter-add x4 -> x0, other arithmetic: 153 us -> none  [the longest x2 119 us: transposed(): jax.ops.segment_sum(partial_terms.reshape(element_count * slot_total, P_S...]
    pallas_call x0 -> x1, Pallas kernels: none -> 146 us  [whole(): pl.pallas_call(whole_kernel, in_specs=[pl.BlockSpec(memory_space=pltpu.SM...]
    all_to_all x8 -> x0, blocking collectives: 120 us -> none  [the longest x5 54.9 us: sent_to_all(): lax.all_to_all(jnp.broadcast_to(x[None], (peers, *x.shape)), axis, 0, 0,...]
    reshape x8 -> x1, local copies, waits for them, and re-layouts: 90.1 us -> 0.1 us  [body(): faces = element_faces.reshape(-1)]
    all_to_all x4 -> x0, waiting for transfers between devices: 50.7 us -> none  [the longest x2 32.6 us: transposed(): lax.all_to_all(reduced[owned_count:].astype(jnp.bfloat16), 'dom', split_a...]
    unnamed x16 -> x6, local copies, waits for them, and re-layouts: 44.3 us -> 1.94 us
    dot_general x2 -> x0, local copies, waits for them, and re-layouts: 32.8 us -> none  [transposed(): jnp.einsum('ekb,ekr->ebr', element_blocks, picked, preferred_element_type...]
    convert_element_type x7 -> x0, other arithmetic: 32.7 us -> none  [the longest x2 17.9 us: transposed(): reduced = sum_at_owner(summed.astype(jnp.bfloat16), 'col', 2)]
  transfers between devices with their start and end apart: 4 -> 0, of which waited for: 4 -> 0; matrix products, arithmetic and copies ran while one was open for 7% -> 0% of each run, Pallas kernels for 0% -> 0%
where the time goes in v1:
time: 158 us; the launch traced here: 157 us
  Pallas kernels  146 us (92%)
  local copies, waits for them, and re-layouts  7.38 us (5%)
  other arithmetic  2.74 us (2%)
    pallas_call x1, Pallas kernels, whole(): pl.pallas_call(whole_kernel, in_specs=[pl.BlockSpec(memory_space=pltpu.SM...  146 us
    transpose x1, local copies, waits for them, and re-layouts, body(): out = lambda x: jnp.transpose(x[:, :, :P_SIZE], (0, 2, 1))  4.08 us

profile of v1, /device:TPU:0, one launch (start us, length us, event | category | flops | bytes accessed | tf_op | source)
XLA Modules:
  0.0 157.3 jit_solution(16941215347879922169)
XLA Ops:
  0.7 0.8 pad_add_fusion.1
  1.4 0.8 select_reduce_fusion.1
  2.3 0.7 fusion.5
  3.0 0.8 copy.8
  3.7 0.1 reshape.15.faces_ref
  3.9 0.0 copy-start
  3.9 0.6 copy-done
  4.4 1.1 select_reduce_fusion
  5.6 0.6 fusion.4
  6.1 146.4 %shard_map.67 = (bf16[192,32,128]{2,1,0:T(8,128)(2,1)}, bf16[192,32,128]{2,1,0:T(8,128)(2,1)}, f32[8,128]{1,0:T(8,128)}) custom-call(s32[192]{0:T(256)} %bitcast.12, s32[384]{0:T(512)} %copy-done, s32[384]{0:T(512)} %get-tuple-element.10.prev_ref, s32[384]{0:T(512)} %get-tuple-element.9.last_ref, s32[192]{0:T(256)} %get-tuple-element.12.prev2_ref, ...), custom_call_target="tpu_custom_call" | custom-call | tf_op jit(solution)/shard_map/pallas_call | solution.py:415
  152.6 0.0 copy-start.1
  152.6 4.1 %slice_bitcast_fusion = (bf16[192,105,32]{1,2,0:T(8,128)(2,1)}, bf16[192,105,32]{1,2,0:T(8,128)(2,1)}) fusion(bf16[192,32,128]{2,1,0:T(8,128)(2,1)} %get-tuple-element.7, bf16[192,32,128]{2,1,0:T(8,128)(2,1)} %get-tuple-element.6), kind=kLoop, calls=%fused_computation | loop fusion | bytes 5160960 | tf_op jit(solution)/shard_map/transpose | solution.py:474
  156.7 0.0 copy-done.1
  156.7 0.6 copy.10
  (7 shorter events, 0.0 us)
Async XLA Ops:
  3.9 0.6 copy-start
  152.6 4.1 %copy-start.1 = (f32[8,128]{1,0:T(8,128)S(1)}, f32[8,128]{1,0:T(8,128)}, u32[]{:S(2)}) copy-start(f32[8,128]{1,0:T(8,128)} %get-tuple-element.8) | copy-start | bytes 12292

commit v2 on v1

--- a/solution.py
+++ b/solution.py
@@ -18,6 +18,9 @@
 ENTRIES = float(NDOM * OWNED * P_SIZE)
 F32 = jnp.float32
 BF16 = jnp.bfloat16
+INVERSE = 19
+LAST = 4 * ELEMS
+LAG = 4
 VMEM_LIMIT = 67043328
 GROUP = 8
 PARTS = 8
@@ -54,8 +57,9 @@
     return cat(parts[0], parts[1]), cat(parts[2], parts[3]), cat(parts[4], tail)
 
 
-def to_lanes(column):
-    return jnp.sum(jnp.where(rows_of(HALF) == lanes(HALF), column, 0.0), axis=0, keepdims=True)
+def to_lanes(column, first):
+    spread = jnp.where(rows_of(HALF) + first == lanes(HALF), column, 0.0)
+    return jnp.sum(spread, axis=0, keepdims=True)
 
 
 def to_rows(row):
@@ -111,7 +115,7 @@
 
 
 def whole_kernel(
-    send_ref, faces_ref, prev_ref, last_ref, prev2_ref, last2_ref, r_ref, a_hbm,
+    send_ref, faces_ref, found_ref, found2_ref, r_ref, a_hbm,
     basis_hbm, next_hbm, h_ref,
     blocks, known, sums, b1, wire, ghost, ghost2, keep, give, got, keepg, giveg, gotg, ret,
     stat, stats, staging,
@@ -173,7 +177,7 @@
             faces = [face(send_ref[SLOT * p + s]) for s in range(SLOT)]
             wire[p] = pack(*faces).astype(BF16)
 
-        loop(0, NDOM, step, 4)
+        return step
 
     def fill(s, source_ref, half):
         for j, face in enumerate(unpack(to_f32(source_ref[s]))):
@@ -184,12 +188,16 @@
         forward(k).start()
         fill(source(k), ghost, 0)
 
+        @pl.when(k > LAG)
+        def _():
+            take_forward(k - LAG)
+
+    def take_forward(k):
+        forward(k).wait_recv()
+        fill(source(k), ghost2, 1)
+
     def halo_end():
-        def step(k):
-            forward(k).wait_recv()
-            fill(source(k), ghost2, 1)
-
-        each(step, 3)
+        loop(NDOM - LAG, NDOM, take_forward)
 
         def done(k):
             send_copy(k).wait_send()
@@ -209,7 +217,7 @@
             )
             y = jnp.dot(x, blocks[e], preferred_element_type=F32)
             for b in range(4):
-                sums[at + b] = y[:, 128 * b : 128 * b + 128] + sums[prev_ref[at + b]]
+                sums[at + b] = y[:, 128 * b : 128 * b + 128] + sums[found_ref[at + b]]
 
         loop(0, ELEMS, element, 8)
         size = NDOM // PARTS
@@ -218,26 +226,11 @@
             def one(j):
                 k = i * size + j
                 p = target(k)
-                t = [sums[last_ref[OWNED + SLOT * p + s]] for s in range(SLOT)]
+                t = [sums[found_ref[LAST + OWNED + SLOT * p + s]] for s in range(SLOT)]
                 keepg[k] = pack(*(x[:HALF] for x in t)).astype(BF16)
                 giveg[k] = pack(*(x[HALF:] for x in t)).astype(BF16)
 
             loop(0, size, one, 4)
-
-            @pl.when(i > 0)
-            def _():
-                cross(i - 1).start()
-
-        loop(0, PARTS, part)
-
-        def take(f):
-            total = sums[last_ref[f]].astype(BF16)
-            keep[f] = total[:HALF]
-            give[f] = total[HALF:]
-
-        loop(0, OWNED, take, 8)
-        cross(PARTS - 1).start()
-        give_copy().start()
 
         def pass_on(i):
             cross(i).wait_recv()
@@ -255,34 +248,56 @@
 
             loop(0, size, go)
 
-        loop(0, PARTS, pass_on)
+        def stage(i):
+            @pl.when(i < PARTS)
+            def _():
+                part(i)
+
+            @pl.when(i >= 3)
+            def _():
+                pass_on(i - 3)
+
+            @pl.when((i > 0) & (i <= PARTS))
+            def _():
+                cross(i - 1).start()
+
+        loop(0, PARTS + 3, stage)
+
+        def take(f):
+            total = sums[found_ref[LAST + f]].astype(BF16)
+            keep[f] = total[:HALF]
+            give[f] = total[HALF:]
+
+        loop(0, OWNED, take, 8)
+        give_copy().start()
 
     def add_returned(image):
+        sums[OWNED, :HALF] = zero
+
+        def step(k):
+            back(k).wait_recv()
+            p = source(k)
+            for s, face in enumerate(unpack(to_f32(ret[p]))):
+                before = sums[found2_ref[SLOT * p + s], :HALF]
+                sums[SLOT * k + s, :HALF] = face + before
+
+        each(step, 3)
+        each(lambda k: back(k).wait_send())
+        loop(0, PARTS, lambda i: cross(i).wait_send())
         give_copy().wait()
-        loop(0, PARTS, lambda i: cross(i).wait_send())
-        each(lambda k: back(k).wait())
-        sums[OWNED, :HALF] = zero
-
-        def step(p):
-            for s, face in enumerate(unpack(to_f32(ret[p]))):
-                at = SLOT * p + s
-                sums[at, :HALF] = face + sums[prev2_ref[at], :HALF]
-
-        loop(0, NDOM, step, 4)
 
         def own(f, carry):
-            value = to_f32(keep[f]) + to_f32(got[f]) + sums[last2_ref[f], :HALF]
+            value = to_f32(keep[f]) + to_f32(got[f]) + sums[found2_ref[OWNED + f], :HALF]
             return image(f, value, carry)
 
         return lax.fori_loop(0, OWNED, own, (zero, zero), unroll=8)
 
     def stat_rows(*columns):
-        stat[...] = jnp.zeros((8, 128), F32)
-        for row, x in enumerate(columns):
-            stat[row : row + 1] = to_lanes(lane_sum(x))
+        stat[...] = sum(to_lanes(lane_sum(x), HALF * i) for i, x in enumerate(columns))
 
     def stat_of(i, row):
-        return stats[i, :, row, :]
+        found = stats[i, :, 0, :]
+        return pltpu.roll(found, 128 - HALF * row, 1) if row else found
 
     def total_of(i, row):
         return jnp.sum(stat_of(i, row), axis=0, keepdims=True)
@@ -306,7 +321,7 @@
         return total + x * x
 
     stat_rows(lax.fori_loop(0, OWNED, enter, zero, unroll=8))
-    pack_faces(right_side)
+    loop(0, NDOM, pack_faces(right_side), 4)
     pl.semaphore_wait(barrier, NDOM)
 
     each(lambda k: send_copy(k).start())
@@ -372,9 +387,24 @@
         keep[f] = b
 
     loop(0, OWNED, second_basis, 8)
-    pack_faces(lambda f: to_f32(keep[f]))
     across().start()
-    each(lambda k: send_copy(k).start())
+    pack_one = pack_faces(lambda f: to_f32(keep[f]))
+
+    def send_some(i):
+        @pl.when(i < 8)
+        def _():
+            loop(0, 8, lambda j: pack_one(target(8 * i + j)), 4)
+
+        @pl.when(i > 0)
+        def _():
+            def go(j):
+                @pl.when(8 * (i - 1) + j > 0)
+                def _():
+                    send_copy(8 * (i - 1) + j).start()
+
+            loop(0, 8, go)
+
+    loop(0, 9, send_some)
     basis = pltpu.make_async_copy(known.at[owned, low], basis_hbm, sem.at[1])
     basis.start()
     each(arrive, 3)
@@ -431,8 +461,8 @@
             vm(message), vm(message), vm(message),
             vm(faces), vm(faces), vm(faces),
             vm(message), vm(message), vm(message), vm(message),
-            vm((8, 128), F32),
-            vm((3, NDOM, 8, 128), F32),
+            vm((1, 128), F32),
+            vm((3, NDOM, 1, 128), F32),
             vm((2, 210, GROUP, 420)),
         ]
         + [sems(2)] + [sems(NDOM)] * 6 + [sems(PARTS)] * 2 + [sems(NDOM)] * 2 + [sems(4), sems(3)],
@@ -442,10 +472,9 @@
     )(*scalars, r, blocks)
 
 
-def latest(names, queries, before, usable, empty):
-    j = jnp.arange(names.shape[0], dtype=jnp.int32)
-    match = (names[None, :] == queries[:, None]) & (j[None, :] < before[:, None]) & usable[None, :]
-    best = jnp.max(jnp.where(match, j[None, :], -1), axis=1)
+def latest(names, order, queries, before, usable, empty):
+    match = (names[None, :] == queries[:, None]) & (order[None, :] < before[:, None])
+    best = jnp.max(jnp.where(match & usable[None, :], order[None, :], -1), axis=1)
     return jnp.where(best < 0, empty, best)
 
 
@@ -458,16 +487,16 @@
     full = jnp.full((2 * OWNED,), 2 * OWNED, jnp.int32)
     every = jnp.ones((faces.shape[0],), bool)
     found = latest(
-        faces, jnp.concatenate([faces, slots]), jnp.concatenate([at, full]), every, 4 * ELEMS
+        faces, at, jnp.concatenate([faces, slots]), jnp.concatenate([at, full]), every, 4 * ELEMS
     )
     owned = slots[:OWNED]
+    partition = owned // SLOT
+    arrival = SLOT * ((INVERSE * (d - partition + NDOM)) % NDOM) + owned % SLOT
     found2 = latest(
-        send, jnp.concatenate([send, owned]), jnp.concatenate([owned, full[:OWNED]]),
-        owned // SLOT != d, OWNED,
+        send, arrival, jnp.concatenate([send, owned]), jnp.concatenate([arrival, full[:OWNED]]),
+        partition != d, OWNED,
     )
-    scalars = (
-        send, faces, found[: 4 * ELEMS], found[4 * ELEMS :], found2[:OWNED], found2[OWNED:],
-    )
+    scalars = (send, faces, found, found2)
     basis, vector, rows = whole(
         scalars, jnp.transpose(adjoint_rhs, (0, 2, 1)), jnp.transpose(element_blocks, (1, 0, 2))
     )

time: 158 us -> 154 us (0.975)
  Pallas kernels: 146 us -> 143 us
    pallas_call x1, Pallas kernels: 146 us -> 143 us  [whole(): pl.pallas_call(whole_kernel, in_specs=[pl.BlockSpec(memory_space=pltpu.SM...]
where the time goes in v2:
time: 154 us
  Pallas kernels  143 us (93%)
  local copies, waits for them, and re-layouts  6.13 us (4%)
  other arithmetic  3.93 us (3%)
    pallas_call x1, Pallas kernels, whole(): pl.pallas_call(whole_kernel, in_specs=[pl.BlockSpec(memory_space=pltpu.SM...  143 us
    transpose x1, local copies, waits for them, and re-layouts, body(): out = lambda x: jnp.transpose(x[:, :, :P_SIZE], (0, 2, 1))  4.08 us

profile of v2, /device:TPU:0, one launch (start us, length us, event | category | flops | bytes accessed | tf_op | source)
XLA Modules:
  0.0 153.7 jit_solution(12818648139270706089)
XLA Ops:
  0.7 0.8 pad_add_fusion.1
  1.5 0.8 select_reduce_fusion.1
  2.3 0.6 compare_select_fusion.1.found2_ref
  2.9 0.8 copy.8
  3.7 0.1 reshape.16.faces_ref
  3.8 0.0 copy-start
  3.8 0.6 copy-done
  4.4 1.1 select_reduce_fusion
  5.5 0.6 compare_select_fusion.found_ref
  6.1 142.9 %shard_map.67 = (bf16[192,32,128]{2,1,0:T(8,128)(2,1)}, bf16[192,32,128]{2,1,0:T(8,128)(2,1)}, f32[8,128]{1,0:T(8,128)}) custom-call(s32[192]{0:T(256)} %bitcast.12, s32[384]{0:T(512)} %copy-done, s32[768]{0:T(1024)} %compare_select_fusion.found_ref, s32[384]{0:T(512)} %compare_select_fusion.1.found2_ref, bf16[192,32,105]{2,1,0:T(8,128)(2,1)} %bitcast.9, ...), custom_call_target="tpu_custom_call" | custom-call | tf_op jit(solution)/shard_map/pallas_call | solution.py:445
  149.0 0.0 copy-start.1
  149.0 4.1 %slice_bitcast_fusion = (bf16[192,105,32]{1,2,0:T(8,128)(2,1)}, bf16[192,105,32]{1,2,0:T(8,128)(2,1)}) fusion(bf16[192,32,128]{2,1,0:T(8,128)(2,1)} %get-tuple-element.7, bf16[192,32,128]{2,1,0:T(8,128)(2,1)} %get-tuple-element.6), kind=kLoop, calls=%fused_computation | loop fusion | bytes 5160960 | tf_op jit(solution)/shard_map/transpose | solution.py:503
  153.1 0.0 copy-done.1
  153.1 0.6 copy.10
  (6 shorter events, 0.1 us)
Async XLA Ops:
  3.8 0.6 copy-start
  149.0 4.1 %copy-start.1 = (f32[8,128]{1,0:T(8,128)S(1)}, f32[8,128]{1,0:T(8,128)}, u32[]{:S(2)}) copy-start(f32[8,128]{1,0:T(8,128)} %get-tuple-element.8) | copy-start | bytes 12292
